TPU v7x, 32 devices: a whole 2x2x4 slice. The times are simulated.
32 devices in a mesh: cols: 2 (over core), space: 16 (over z, y, x).
Axes of the slice: x: 2, y: 2, z: 4, core: 2. Of those that a mesh axis runs over, the one named last changes fastest.
Arguments:
- mean_state: float32 [6, 256, 256], P(None, 'space', 'cols'), may hold values from -2 to 2
- covariance: float32 [128, 6, 256, 256], P('cols', None, 'space'), may hold values from -2 to 2
- land_mask: int32 [256, 256], replicated, may hold values 0 or 1
- stations: int32 [2048], P('space'), may hold values from 0 to 65535, as said below
- observed: float32 [2048], P('space'), may hold values from -5 to 5
- obs_weight: float32 [2048], P('space'), may hold values from 0.5 to 4
Outputs:
- mean_analysis: float32 [6, 256, 256], P(None, 'space', 'cols')
- covariance_analysis: float32 [128, 6, 256, 256], P('cols', None, 'space')
Inputs may be any that keep to these rules, and one draw needn't show every extreme that they name: Stations b * 128 to (b + 1) * 128 - 1 lie in grid rows b * 16 to (b + 1) * 16 - 1; several stations may share a cell.
All inputs are finite; a program needn't handle non-finite values.
Results may differ from a plain program's by a relative error of at most 0.0053.
Values may be sent and summed in bfloat16 or wider, within the bound.
No kernel may reach another device: no remote copies, remote signals or barrier semaphores. Data moves between devices by JAX's collectives and lax.ppermute only.
A program may use at most 128 MiB of HBM per device.

v0:
```python
import jax
import jax.numpy as jnp
from jax import lax
from jax.sharding import PartitionSpec as P

ITERS = 4
time_step = 0.5
gravity = 1.0
reduced_gravity = 0.125
coriolis = 0.3
friction = 0.05
layer_depths = (1.0, 2.0)


def padded_2(block, sides, width):
    for axis, dim in sides:
        count = lax.axis_size(axis)
        forward = [(i, i + 1) for i in range(count - 1)]
        backward = [(target, source) for source, target in forward]
        low = lax.ppermute(
            lax.slice_in_dim(block, block.shape[dim] - width, None, axis=dim), axis, forward
        )
        high = lax.ppermute(lax.slice_in_dim(block, 0, width, axis=dim), axis, backward)
        block = jnp.concatenate([low, block, high], axis=dim)
    return block


def diff_rows(values):
    return 0.5 * (values[..., 2:, 1:-1] - values[..., :-2, 1:-1])


def diff_cols(values):
    return 0.5 * (values[..., 1:-1, 2:] - values[..., 1:-1, :-2])


def inner(values):
    return values[..., 1:-1, 1:-1]


def velocities(field, wet_cells):
    wet_inner = inner(wet_cells)
    surface = field[..., 0, :, :] + field[..., 3, :, :]
    pressure_top = gravity * surface
    pressure_pair = (pressure_top, pressure_top - reduced_gravity * field[..., 0, :, :])
    velocity_pairs = []
    for layer_index in range(2):
        zonal = inner(field[..., 3 * layer_index + 1, :, :])
        north = inner(field[..., 3 * layer_index + 2, :, :])
        pressure = pressure_pair[layer_index]
        zonal_new = wet_inner * (
            zonal + time_step * (-diff_rows(pressure) + coriolis * north - friction * zonal)
        )
        north_new = wet_inner * (
            north + time_step * (-diff_cols(pressure) - coriolis * zonal - friction * north)
        )
        velocity_pairs.append((zonal_new, north_new))
    return velocity_pairs


def mean_core(padded, wet_cells):
    velocity_pairs = velocities(padded, wet_cells)
    fields = []
    carried = []
    for layer_index in range(2):
        thickness = padded[3 * layer_index]
        column_depth = layer_depths[layer_index] + inner(thickness)
        zonal_new, north_new = velocity_pairs[layer_index]
        updated = thickness[2:-2, 2:-2] - time_step * (
            diff_rows(column_depth * zonal_new) + diff_cols(column_depth * north_new)
        )
        fields += [updated, zonal_new[1:-1, 1:-1], north_new[1:-1, 1:-1]]
        carried += [thickness[1:-1, 2:-2], zonal_new[:, 1:-1], north_new[:, 1:-1]]
    return (jnp.stack(fields), jnp.stack(carried))


def tangent_core(padded, carried, wet_cells):
    beside_all = jnp.pad(carried, ((0, 0), (0, 0), (1, 1)))
    velocity_pairs = velocities(padded, wet_cells)
    fields = []
    for layer_index in range(2):
        thickness = padded[..., 3 * layer_index, :, :]
        column_depth = layer_depths[layer_index] + beside_all[3 * layer_index]
        zonal_new, north_new = velocity_pairs[layer_index]
        flux_rows = column_depth * zonal_new + inner(thickness) * beside_all[3 * layer_index + 1]
        flux_cols = column_depth * north_new + inner(thickness) * beside_all[3 * layer_index + 2]
        updated = thickness[..., 2:-2, 2:-2] - time_step * (
            diff_rows(flux_rows) + diff_cols(flux_cols)
        )
        fields += [updated, zonal_new[..., 1:-1, 1:-1], north_new[..., 1:-1, 1:-1]]
    return jnp.stack(fields, axis=-3)


def local(mean_state, covariance, land_mask, stations, observed, obs_weight):
    local_cols = covariance.shape[0]
    tile_rows = covariance.shape[2]
    grid_cols = covariance.shape[3]
    piece_cols = mean_state.shape[2]
    total_cols = local_cols * lax.axis_size("cols")
    space_index = lax.axis_index("space")
    column_index = lax.axis_index("cols")
    land_float = land_mask.astype(jnp.float32)
    first_row = space_index * tile_rows
    columns = covariance
    depth = 2 * ITERS
    grid_rows = tile_rows * lax.axis_size("space")
    mean_now = lax.all_gather(mean_state, "cols", axis=2, tiled=True)
    mean_now = padded_2(mean_now, (("space", 1),), depth)
    columns = padded_2(columns, (("space", 2),), depth)
    wet_deep = jnp.pad(land_float, ((depth, depth), (2, 2)))
    rows_here = first_row - depth + jnp.arange(tile_rows + 2 * depth, dtype=jnp.int32)
    inside = jnp.logical_and(rows_here >= 0, rows_here < grid_rows).astype(jnp.float32)
    for step_index in range(ITERS):
        extent = depth - 2 * step_index
        shrink = 2 * step_index
        wet_cells = lax.dynamic_slice_in_dim(
            wet_deep, first_row + shrink, tile_rows + 2 * extent, 0
        )
        padded_mean = jnp.pad(mean_now, ((0, 0), (0, 0), (2, 2)))
        mean_next, carried = mean_core(padded_mean, wet_cells)
        padded_columns = jnp.pad(columns, ((0, 0), (0, 0), (0, 0), (2, 2)))
        columns_next = tangent_core(padded_columns, carried, wet_cells)
        keep = inside[shrink + 2 : shrink + 2 + tile_rows + 2 * (extent - 2)]
        mean_now = mean_next * keep[None, :, None]
        columns = columns_next * keep[:, None]
    mean_piece = lax.dynamic_slice_in_dim(mean_now, column_index * piece_cols, piece_cols, 2)
    surface = mean_now[0] + mean_now[3]
    offset_stations = stations - first_row * grid_cols
    column_surface = (columns[:, 0] + columns[:, 3]).reshape(local_cols, tile_rows * grid_cols)
    sensed_local = jnp.take(column_surface, offset_stations, axis=1) * obs_weight[None, :]
    innovation = obs_weight * (observed - jnp.take(surface.reshape(-1), offset_stations))
    sensed = lax.all_gather(sensed_local, "cols", axis=0, tiled=True)
    products = jnp.dot(
        sensed, sensed.T, precision=lax.Precision.HIGHEST, preferred_element_type=jnp.float32
    )
    target_part = jnp.dot(
        sensed, innovation, precision=lax.Precision.HIGHEST, preferred_element_type=jnp.float32
    )
    gram_sum, target = lax.psum((products, target_part), "space")
    identity = jnp.eye(total_cols, dtype=jnp.float32)
    gram_matrix = identity + gram_sum
    lower_factor = lax.linalg.cholesky(gram_matrix)
    halfway = lax.linalg.triangular_solve(lower_factor, target[:, None], left_side=True, lower=True)
    weights = lax.linalg.triangular_solve(
        lower_factor, halfway, left_side=True, lower=True, transpose_a=True
    )[:, 0]
    inverse = lax.linalg.triangular_solve(lower_factor, identity, left_side=True, lower=True)
    transform_low = inverse.T.astype(jnp.bfloat16)
    weights_local = lax.dynamic_slice_in_dim(weights, column_index * local_cols, local_cols)
    increment_terms = jnp.einsum(
        "k,kfrc->frc", weights_local, columns, precision=lax.Precision.HIGHEST
    )
    increment_total = lax.psum(increment_terms, "cols")
    increment = lax.dynamic_slice_in_dim(increment_total, column_index * piece_cols, piece_cols, 2)
    columns_low = columns.astype(jnp.bfloat16)
    shard_piece = lax.all_gather(columns_low, "cols", axis=0, tiled=True)
    transform_part = lax.dynamic_slice(
        transform_low, (0, column_index * local_cols), (shard_piece.shape[0], local_cols)
    )
    updated = jnp.einsum(
        "kj,kfrc->jfrc", transform_part, shard_piece, preferred_element_type=jnp.float32
    )
    return (mean_piece + increment, updated)


def solution(mesh):
    return jax.shard_map(
        local,
        mesh=mesh,
        in_specs=(
            P(None, "space", "cols"),
            P("cols", None, "space", None),
            P(),
            P("space"),
            P("space"),
            P("space"),
        ),
        out_specs=(P(None, "space", "cols"), P("cols", None, "space", None)),
        check_vma=False,
    )
```

profile of v0, /device:TPU:0, one launch (start us, length us, event | category | flops | bytes accessed | tf_op | source)
XLA Modules:
  0.0 518.4 jit_solution(15029220077060353122)
XLA Ops:
  7.2 6.4 %copy.20 = f32[64,6,16,256]{3,0,2,1:T(8,128)S(1)} copy(f32[64,6,16,256]{3,2,1,0:T(8,128)} %param.7) | data formatting | bytes 12582912 | tf_op args[1]
  13.6 2.6 fusion.460
  16.3 1.0 copy-done
  17.2 1.3 collective-permute-start.3
  18.5 7.3 %collective-permute-start.2 = (f32[64,6,8,256]{3,0,2,1:T(8,128)S(1)}, f32[64,6,8,256]{3,0,2,1:T(8,128)}, u32[]{:S(2)}, u32[]{:S(2)}) collective-permute-start(f32[64,6,8,256]{3,0,2,1:T(8,128)S(1)} %get-tuple-element.128), channel_id=1, source_target_pairs={{0,1},{1,2},{2,3},{3,4},{4,5},{5,6},{6,7},{7,8},{8,9},{9,10},{10,1... | collective-permute-start | bytes 9437192 | tf_op jit(solution)/shard_map/ppermute | solution.py:20
  25.8 1.9 all_gather.9
  28.3 1.3 collective-permute-start.1
  29.6 5.2 collective-permute-start
  38.9 1.0 convert_element_type.41
  39.9 119.6 %collective-permute-done.1 = f32[6,8,256]{2,1,0:T(8,128)} collective-permute-done((f32[6,8,256]{2,1,0:T(8,128)}, f32[6,8,256]{2,1,0:T(8,128)}, u32[]{:S(2)}, u32[]{:S(2)}) %collective-permute-start.1) | collective-permute-done | bytes 49184 | tf_op jit(solution)/shard_map/ppermute | solution.py:23
  159.5 1.4 collective-permute-done
  160.9 1.0 select_maximum_fusion.2
  168.1 2.0 gather_fusion.1
  170.1 1.6 fusion.298
  171.8 1.6 fusion.306
  181.5 9.8 %select_maximum_fusion = f32[64,6,32,260]{3,0,2,1:T(8,128)S(1)} fusion(f32[64,6,8,256]{3,0,2,1:T(8,128)} %collective-permute-done.3, f32[64,6,16,256]{3,0,2,1:T(8,128)} %copy-done, f32[64,6,8,256]{3,0,2,1:T(8,128)} %collective-permute-done.2), kind=kLoop, calls=%fused_computation.16 | loop fusion | flops 25559040 | bytes 25362432 | tf_op jit(solution)/shard_map/concatenate | solution.py:24
  191.4 6.6 %slice_bitcast_fusion = (f32[64,32,260]{2,0,1:T(8,128)}, f32[64,32,260]{2,0,1:T(8,128)}, f32[64,32,260]{2,0,1:T(8,128)}, f32[64,32,260]{2,0,1:T(8,128)}, f32[64,32,260]{2,0,1:T(8,128)}, /*index=5*/f32[64,32,260]{2,0,1:T(8,128)}) fusion(f32[64,6,32,260]{3,0,2,1:T(8,128)S(1)} %select_maximum_fusion), kind=kLoop, calls=%fused_computation.28 | loop fusion | bytes 25559040 | tf_op jit(solution)/shard_map/squeeze | solution.py:48
  198.0 2.2 multiply_subtract_fusion
  200.3 12.8 %multiply_add_fusion.3 = (f32[64,30,258]{2,0,1:T(8,128)S(1)}, f32[64,30,258]{2,0,1:T(8,128)}, f32[64,30,258]{2,0,1:T(8,128)S(1)}, f32[64,30,258]{2,0,1:T(8,128)S(1)}) fusion(f32[64,32,260]{2,0,1:T(8,128)} %get-tuple-element.85, f32[30,258]{1,0:T(8,128)S(1)} %copy-done.51, f32[30,258]{1,0:T(8,128)S(1)} %copy-done.53, f32[64,32,260]{2,0,1:T(8,128)} %get-tuple-element.82, ...), kind=kLoop, calls=%fused_computation.71 | loop fusion | flops 12879360 | bytes 21919680 | tf_op jit(solution)/shard_map/add | solution.py:84
  213.2 3.2 fusion.116
  216.3 1.8 fusion.111
  218.1 1.8 fusion.110
  219.9 0.9 copy-done.2
  220.9 6.3 %multiply_add_fusion.1 = (f32[64,30,258]{2,0,1:T(8,128)S(1)}, f32[64,30,258]{2,0,1:T(8,128)}, f32[64,30,258]{2,0,1:T(8,128)S(1)}, f32[64,30,258]{2,0,1:T(8,128)S(1)}) fusion(f32[64,32,260]{2,0,1:T(8,128)S(1)} %copy-done.2, f32[30,258]{1,0:T(8,128)S(1)} %copy-done.48, f32[30,258]{1,0:T(8,128)S(1)} %copy-done.49, f32[64,32,260]{2,0,1:T(8,128)S(1)} %copy-done.4, ...), kind=kLoop, calls=%fused_computation.69 | loop fusion | flops 12879360 | bytes 21919680 | tf_op jit(solution)/shard_map/add | solution.py:84
  227.2 3.3 fusion.109
  230.4 1.8 fusion.104
  232.2 1.8 fusion.103
  234.0 6.5 %broadcast_multiply_fusion = f32[64,6,28,256]{3,0,2,1:T(8,128)S(1)} fusion(f32[64,6,28,256]{3,0,2,1:T(8,128)} %fusion.103, f32[28]{0:T(128)S(1)} %copy-done.73), kind=kLoop, calls=%fused_computation.25 | loop fusion | flops 2752512 | bytes 22020208 | tf_op jit(solution)/shard_map/mul | solution.py:124
  240.5 6.7 %fusion.34 = (f32[64,28,260]{2,0,1:T(8,128)}, f32[64,28,260]{2,0,1:T(8,128)}, f32[64,28,260]{2,0,1:T(8,128)S(1)}, f32[64,28,260]{2,0,1:T(8,128)}, f32[64,28,260]{2,0,1:T(8,128)}, /*index=5*/f32[64,28,260]{2,0,1:T(8,128)S(1)}) fusion(f32[64,6,28,256]{3,0,2,1:T(8,128)S(1)} %broadcast_multiply_fusion), kind=kLoop, calls=%fused_computation.77 | loop fusion | bytes 22192128 | tf_op jit(solution)/shard_map/squeeze | solution.py:48
  247.3 2.9 multiply_subtract_fusion.1
  250.2 8.1 %multiply_add_fusion.7 = (f32[64,26,258]{2,0,1:T(8,128)S(1)}, f32[64,26,258]{2,0,1:T(8,128)}, f32[64,26,258]{2,0,1:T(8,128)S(1)}, f32[64,26,258]{2,0,1:T(8,128)}) fusion(f32[64,28,260]{2,0,1:T(8,128)S(1)} %get-tuple-element.101, f32[26,258]{1,0:T(8,128)S(1)} %copy-done.45, f32[26,258]{1,0:T(8,128)S(1)} %copy-done.47, f32[64,28,260]{2,0,1:T(8,128)} %get-tuple-element.99, ...), kind=kLoop, calls=%fused_computation.114 | loop fusion | flops 11162112 | bytes 18997056 | tf_op jit(solution)/shard_map/add | solution.py:84
  258.3 1.8 fusion.158
  262.8 5.8 %multiply_add_fusion.5 = (f32[64,26,258]{2,0,1:T(8,128)S(1)}, f32[64,26,258]{2,0,1:T(8,128)}, f32[64,26,258]{2,0,1:T(8,128)S(1)}, f32[64,26,258]{2,0,1:T(8,128)}) fusion(f32[64,28,260]{2,0,1:T(8,128)S(1)} %get-tuple-element.98, f32[26,258]{1,0:T(8,128)S(1)} %get-tuple-element.142, f32[26,258]{1,0:T(8,128)S(1)} %get-tuple-element.145, ...), kind=kLoop, calls=%fused_computation.112 | loop fusion | flops 11162112 | bytes 18997056 | tf_op jit(solution)/shard_map/add | solution.py:84
  268.6 1.7 fusion.151
  270.8 1.2 copy-done.15
  272.5 2.1 broadcast_multiply_fusion.1
  274.6 4.0 fusion.68
  278.6 2.5 multiply_subtract_fusion.2
  281.2 5.8 %multiply_add_fusion.11 = (f32[64,22,258]{2,0,1:T(8,128)S(1)}, f32[64,22,258]{2,0,1:T(8,128)}, f32[64,22,258]{2,0,1:T(8,128)S(1)}, f32[64,22,258]{2,0,1:T(8,128)}) fusion(f32[64,24,260]{2,0,1:T(8,128)S(1)} %get-tuple-element.113, f32[22,258]{1,0:T(8,128)S(1)} %copy-done.57, f32[22,258]{1,0:T(8,128)} %get-tuple-element.185, ...), kind=kLoop, calls=%fused_computation.157 | loop fusion | flops 9444864 | bytes 16074432 | tf_op jit(solution)/shard_map/add | solution.py:84
  286.9 1.5 fusion.172
  289.0 1.1 copy-done.19
  290.5 3.9 multiply_add_fusion.9
  294.4 1.4 fusion.165
  296.7 1.3 broadcast_multiply_fusion.2
  297.9 7.0 %fusion.102 = (f32[64,20,260]{2,0,1:T(8,128)}, f32[64,20,260]{2,0,1:T(8,128)}, f32[64,20,260]{2,0,1:T(8,128)S(1)}, f32[64,20,260]{2,0,1:T(8,128)}, f32[64,20,260]{2,0,1:T(8,128)}, /*index=5*/f32[64,20,260]{2,0,1:T(8,128)}) fusion(f32[64,6,20,256]{3,0,2,1:T(8,128)S(1)} %broadcast_multiply_fusion.2), kind=kLoop, calls=%fused_computation.163 | loop fusion | bytes 15851520 | tf_op jit(solution)/shard_map/squeeze | solution.py:48
  304.9 2.1 multiply_subtract_fusion.3
  307.6 3.0 multiply_add_fusion.15
  310.7 1.2 fusion.186
  314.1 3.5 multiply_add_fusion.13
  317.6 1.2 fusion.179
  319.4 3.2 fusion.427
  322.7 2.7 copy-done.1
  327.1 1.9 all_gather.10
  329.0 0.9 fusion.463
  330.2 41.4 %psum.22 = f32[128]{0:T(128)S(1)} all-reduce(f32[128]{0:T(128)S(1)} %convolution_bitcast_fusion.2), channel_id=1, replica_groups=mesh['cols'=2,'space'=16] {'space'}, use_global_device_ids=true, to_apply=%region_3.4 | all-reduce | flops 128 | bytes 1024 | tf_op jit(solution)/shard_map/psum | solution.py:138
  371.6 62.5 %all-reduce.16.cloned.1.call-done = f32[128,128]{1,0:T(8,128)} async-done(((f32[128,128]{1,0:T(8,128)}), f32[128,128]{1,0:T(8,128)}) %all-reduce.16.cloned.1.call-update) | async-done | bytes 65552 | tf_op jit(solution)/shard_map/psum | solution.py:138
  435.9 11.7 %cholesky.18 = f32[128,128]{1,0:T(8,128)S(1)} custom-call(f32[128,128]{1,0:T(8,128)S(1)} %fusion.193), custom_call_target="Cholesky" | custom-call | tf_op jit(solution)/shard_map/cholesky | solution.py:141
  449.0 9.8 %custom-call.9 = f32[1,128,128]{1,2,0:T(8,128)S(1)} custom-call(f32[1,128,128]{2,1,0:T(8,128)S(1)} %fusion.188), custom_call_target="InvertDiagBlocksLowerTriangular" | custom-call | tf_op jit(solution)/shard_map/triangular_solve | solution.py:143
  459.1 5.1 fusion.409
  465.9 16.0 %all-reduce.18.cloned.1.call-done = f32[6,16,256]{2,1,0:T(8,128)} async-done(((f32[6,16,256]{2,1,0:T(8,128)}), f32[6,16,256]{2,1,0:T(8,128)}) %all-reduce.18.cloned.1.call-update) | async-done | bytes 98320 | tf_op jit(solution)/shard_map/psum | solution.py:152
  482.0 1.4 dynamic-slice_add_fusion
  483.4 18.1 %all-gather.2.cloned.1.call-done = bf16[128,6,16,256]{3,0,2,1:T(8,128)(2,1)} async-done(((bf16[64,6,16,256]{3,0,2,1:T(8,128)(2,1)}), bf16[128,6,16,256]{3,0,2,1:T(8,128)(2,1)}) %all-gather.2.cloned.1.call-update) | async-done | bytes 6291472 | tf_op jit(solution)/shard_map/all_gather | solution.py:155
  501.5 3.8 fusion.397
  505.3 6.3 %copy.27 = f32[64,6,16,256]{3,2,1,0:T(8,128)} copy(f32[64,6,16,256]{3,0,2,1:T(8,128)S(1)} %fusion.397) | data formatting | bytes 12582912
  (273 shorter events, 34.8 us)
Async XLA Ops:
  7.2 426.9 %all-reduce.16.cloned.1.call-start = ((), (), s32[]{:S(2)}) async-start(), calls=%async_computation | async-start | bytes 131072 | tf_op jit(solution)/shard_map/psum | solution.py:138
  13.6 3.7 copy-start
  13.6 12.2 %copy-start.65 = (f32[6,16,128]{2,1,0:T(8,128)S(1)}, f32[6,16,128]{2,1,0:T(8,128)}, u32[]{:S(2)}) copy-start(f32[6,16,128]{2,1,0:T(8,128)} %param.6) | copy-start | bytes 147460
  13.6 21.1 %copy-start.80 = (s32[128]{0:T(128)S(1)}, s32[128]{0:T(128)}, u32[]{:S(2)}) copy-start(s32[128]{0:T(128)} %param.9) | copy-start | bytes 1540
  17.2 164.3 %collective-permute-start.3 = (f32[64,6,8,256]{3,0,2,1:T(8,128)}, f32[64,6,8,256]{3,0,2,1:T(8,128)}, u32[]{:S(2)}, u32[]{:S(2)}) collective-permute-start(f32[64,6,8,256]{3,0,2,1:T(8,128)} %get-tuple-element.129), channel_id=1, source_target_pairs={{1,0},{2,1},{3,2},{4,3},{5,4},{6,5},{7,6},{8,7},{9,8},{10,9},{11,1... | collective-permute-start | bytes 9437192 | tf_op jit(solution)/shard_map/ppermute | solution.py:23
  18.5 163.0 %collective-permute-start.2 = (f32[64,6,8,256]{3,0,2,1:T(8,128)S(1)}, f32[64,6,8,256]{3,0,2,1:T(8,128)}, u32[]{:S(2)}, u32[]{:S(2)}) collective-permute-start(f32[64,6,8,256]{3,0,2,1:T(8,128)S(1)} %get-tuple-element.128), channel_id=1, source_target_pairs={{0,1},{1,2},{2,3},{3,4},{4,5},{5,6},{6,7},{7,8},{8,9},{9,10},{10,1... | collective-permute-start | bytes 9437192 | tf_op jit(solution)/shard_map/ppermute | solution.py:20
  28.3 131.2 %collective-permute-start.1 = (f32[6,8,256]{2,1,0:T(8,128)}, f32[6,8,256]{2,1,0:T(8,128)}, u32[]{:S(2)}, u32[]{:S(2)}) collective-permute-start(f32[6,8,256]{2,1,0:T(8,128)} %get-tuple-element.195), channel_id=1, source_target_pairs={{1,0},{2,1},{3,2},{4,3},{5,4},{6,5},{7,6},{8,7},{9,8},{10,9},{11,1... | collective-permute-start | bytes 147464 | tf_op jit(solution)/shard_map/ppermute | solution.py:23
  29.6 131.3 %collective-permute-start = (f32[6,8,256]{2,1,0:T(8,128)S(1)}, f32[6,8,256]{2,1,0:T(8,128)}, u32[]{:S(2)}, u32[]{:S(2)}) collective-permute-start(f32[6,8,256]{2,1,0:T(8,128)S(1)} %get-tuple-element.194), channel_id=1, source_target_pairs={{0,1},{1,2},{2,3},{3,4},{4,5},{5,6},{6,7},{7,8},{8,9},{9,10},{10,1... | collective-permute-start | bytes 147464 | tf_op jit(solution)/shard_map/ppermute | solution.py:20
  39.9 123.0 %copy-start.72 = (f32[28]{0:T(128)S(1)}, f32[28]{0:T(128)}, u32[]{:S(2)}) copy-start(f32[28]{0:T(128)} %slice.1097) | copy-start | bytes 340
  162.1 2.2 copy-start.21
  162.1 2.2 copy-start.35
  162.3 2.5 copy-start.32
  162.3 2.5 copy-start.33
  162.3 2.5 copy-start.34
  163.1 2.4 copy-start.28
  163.1 2.4 copy-start.70
  163.4 2.6 copy-start.41
  163.7 3.0 copy-start.36
  163.7 3.0 copy-start.38
  163.7 3.0 copy-start.40
  164.4 3.1 copy-start.68
  166.5 12.2 %copy-start.29 = (f32[28,260]{1,0:T(8,128)S(1)}, f32[28,260]{1,0:T(8,128)}, u32[]{:S(2)}) copy-start(f32[28,260]{1,0:T(8,128)} %copy-done.28) | copy-start | bytes 87364
  166.7 12.9 %copy-start.39 = (f32[26,258]{1,0:T(8,128)S(1)}, f32[26,258]{1,0:T(8,128)}, u32[]{:S(2)}) copy-start(f32[26,258]{1,0:T(8,128)} %copy-done.38) | copy-start | bytes 80500
  166.7 13.9 %copy-start.37 = (f32[26,258]{1,0:T(8,128)S(1)}, f32[26,258]{1,0:T(8,128)}, u32[]{:S(2)}) copy-start(f32[26,258]{1,0:T(8,128)} %copy-done.36) | copy-start | bytes 80500
  167.7 13.9 %copy-start.30 = (f32[6,16,256]{2,1,0:T(8,128)}, f32[6,16,256]{2,1,0:T(8,128)S(1)}, u32[]{:S(2)}) copy-start(f32[6,16,256]{2,1,0:T(8,128)S(1)} %broadcast_multiply_fusion.7) | copy-start | bytes 294916
  198.0 2.3 copy-start.22
  198.0 2.3 copy-start.51
  198.0 2.3 copy-start.52
  198.0 2.3 copy-start.53
  200.3 12.8 %copy-start.3 = (f32[64,32,260]{2,0,1:T(8,128)S(1)}, f32[64,32,260]{2,0,1:T(8,128)}, u32[]{:S(2)}) copy-start(f32[64,32,260]{2,0,1:T(8,128)} %get-tuple-element.85) | copy-start | bytes 6389764
  213.1 3.2 copy-start.10
  213.1 6.8 %copy-start.5 = (f32[64,32,260]{2,0,1:T(8,128)S(1)}, f32[64,32,260]{2,0,1:T(8,128)}, u32[]{:S(2)}) copy-start(f32[64,32,260]{2,0,1:T(8,128)} %get-tuple-element.81) | copy-start | bytes 6389764
  216.3 3.6 copy-start.4
  218.1 2.7 copy-start.2
  218.1 2.7 copy-start.48
  218.1 2.7 copy-start.49
  218.1 2.7 copy-start.50
  227.2 3.3 copy-start.9
  247.3 2.9 copy-start.45
  247.3 2.9 copy-start.46
  247.3 2.9 copy-start.47
  258.3 2.5 copy-start.16
  260.1 2.7 copy-start.8
  260.1 2.7 copy-start.44
  270.3 2.2 copy-start.76
  278.6 2.5 copy-start.24
  278.6 2.5 copy-start.57
  278.6 2.5 copy-start.58
  304.9 2.1 copy-start.6
  304.9 2.1 copy-start.13
  304.9 2.7 copy-start.14
  304.9 2.7 copy-start.26
  304.9 2.7 copy-start.62
  304.9 2.7 copy-start.63
  304.9 2.7 copy-start.64
  311.9 2.1 copy-start.12
  311.9 2.1 copy-start.59
  322.7 2.7 copy-start.1
  325.5 4.4 copy-start.67
  325.5 4.4 copy-start.78
  325.5 4.4 copy-start.79
  329.9 152.1 %all-reduce.18.cloned.1.call-start = ((), (), s32[]{:S(2)}) async-start(), calls=%async_computation.1 | async-start | bytes 196608 | tf_op jit(solution)/shard_map/psum | solution.py:152
  464.3 17.7 %copy-start.31 = (f32[6,16,256]{2,1,0:T(8,128)S(1)}, f32[6,16,256]{2,1,0:T(8,128)}, u32[]{:S(2)}) copy-start(f32[6,16,256]{2,1,0:T(8,128)} %copy-done.30) | copy-start | bytes 294916
  464.9 36.6 %all-gather.2.cloned.1.call-start = ((), (), s32[]{:S(2)}) async-start(), calls=%async_computation.2 | async-start | bytes 9437184 | tf_op jit(solution)/shard_map/all_gather | solution.py:155
  (24 other events, 36.9 us)
Sparse Core Ops, SparseCore 0:
  330.0 104.0 all-reduce.15
  465.1 16.8 all-reduce.17
  483.5 17.9 all-gather.1
where the time goes:
time: 526 us; the launch traced here: 518 us
  waiting for transfers between devices  218 us (41%)
  other arithmetic  134 us (25%)
  local copies, waits for them, and re-layouts  80.1 us (15%)
  blocking collectives  45.1 us (9%)
  starting transfers between devices  15.3 us (3%)
  between operations  15.2 us (3%)
  matrix products  10.6 us (2%)
    ppermute x2, waiting for transfers between devices, padded_2(): lax.ppermute(lax.slice_in_dim(block, 0, width, axis=dim), axis, backward)  120 us
    psum x1, waiting for transfers between devices, local(): gram_sum, target = lax.psum((products, target_part), 'space')  62.5 us
    add x8, other arithmetic, tangent_core(): column_depth * zonal_new  49.2 us
    psum x1, blocking collectives, local(): gram_sum, target = lax.psum((products, target_part), 'space')  41.4 us
    unnamed x209, local copies, waits for them, and re-layouts  41.1 us
    squeeze x4, local copies, waits for them, and re-layouts, velocities(): north = inner(field[..., 3 * layer_index + 2, :, :])  24.3 us
    all_gather x1, waiting for transfers between devices, local(): shard_piece = lax.all_gather(columns_low, 'cols', axis=0, tiled=True)  18.1 us
    psum x1, waiting for transfers between devices, local(): increment_total = lax.psum(increment_terms, 'cols')  16 us
  transfers between devices with their start and end apart: 7, of which 5 were waited for; matrix products, arithmetic and copies ran while one was open for 5% of the time, Pallas kernels for 0%

commit v1 on v0

--- a/solution.py
+++ b/solution.py
@@ -149,7 +149,7 @@
     increment_terms = jnp.einsum(
         "k,kfrc->frc", weights_local, columns, precision=lax.Precision.HIGHEST
     )
-    increment_total = lax.psum(increment_terms, "cols")
+    increment_total = jnp.sum(lax.all_gather(increment_terms, "cols"), axis=0)
     increment = lax.dynamic_slice_in_dim(increment_total, column_index * piece_cols, piece_cols, 2)
     columns_low = columns.astype(jnp.bfloat16)
     shard_piece = lax.all_gather(columns_low, "cols", axis=0, tiled=True)

time: 526 us -> 484 us (0.920)
  waiting for transfers between devices: 218 us -> 177 us
    all_gather x1, waiting for transfers between devices: 18.1 us -> 0.03 us  [local(): shard_piece = lax.all_gather(columns_low, 'cols', axis=0, tiled=True)]
    psum x1 -> x0, waiting for transfers between devices: 16 us -> none  [local(): increment_total = lax.psum(increment_terms, 'cols')]
    psum x1, waiting for transfers between devices: 62.5 us -> 55.5 us  [local(): gram_sum, target = lax.psum((products, target_part), 'space')]
    unnamed x209 -> x187, local copies, waits for them, and re-layouts: 41.1 us -> 38.1 us
    unnamed x17 -> x18, other arithmetic: 16 us -> 17.5 us
  transfers between devices with their start and end apart: 7 -> 6, of which waited for: 5 -> 3; matrix products, arithmetic and copies ran while one was open for 5% -> 11% of each run, Pallas kernels for 0% -> 0%
where the time goes in v1:
time: 484 us; the launch traced here: 477 us
  waiting for transfers between devices  177 us (37%)
  other arithmetic  134 us (28%)
  local copies, waits for them, and re-layouts  75.7 us (16%)
  blocking collectives  47.3 us (10%)
  between operations  16.7 us (3%)
  starting transfers between devices  15.1 us (3%)
  matrix products  10.6 us (2%)
    ppermute x2, waiting for transfers between devices, padded_2(): lax.ppermute(lax.slice_in_dim(block, 0, width, axis=dim), axis, backward)  120 us
    psum x1, waiting for transfers between devices, local(): gram_sum, target = lax.psum((products, target_part), 'space')  55.5 us
    add x8, other arithmetic, tangent_core(): column_depth * zonal_new  49.2 us
    psum x1, blocking collectives, local(): gram_sum, target = lax.psum((products, target_part), 'space')  41.4 us
    unnamed x187, local copies, waits for them, and re-layouts  38.1 us
    squeeze x4, local copies, waits for them, and re-layouts, velocities(): north = inner(field[..., 3 * layer_index + 2, :, :])  24.3 us
    unnamed x18, other arithmetic  17.5 us
    ppermute x2, starting transfers between devices, padded_2(): lax.ppermute(lax.slice_in_dim(block, block.shape[dim] - width, None, axis...  12.4 us
  transfers between devices with their start and end apart: 6, of which 3 were waited for; matrix products, arithmetic and copies ran while one was open for 11% of the time, Pallas kernels for 0%

profile of v1, /device:TPU:0, one launch (start us, length us, event | category | flops | bytes accessed | tf_op | source)
XLA Modules:
  0.0 476.5 jit_solution(11927369375241534054)
XLA Ops:
  8.0 6.4 %copy.20 = f32[64,6,16,256]{3,0,2,1:T(8,128)S(1)} copy(f32[64,6,16,256]{3,2,1,0:T(8,128)} %param.7) | data formatting | bytes 12582912 | tf_op args[1]
  14.4 2.6 fusion.460
  17.1 1.0 copy-done
  18.1 1.3 collective-permute-start.3
  19.3 7.3 %collective-permute-start.2 = (f32[64,6,8,256]{3,0,2,1:T(8,128)S(1)}, f32[64,6,8,256]{3,0,2,1:T(8,128)}, u32[]{:S(2)}, u32[]{:S(2)}) collective-permute-start(f32[64,6,8,256]{3,0,2,1:T(8,128)S(1)} %get-tuple-element.128), channel_id=1, source_target_pairs={{0,1},{1,2},{2,3},{3,4},{4,5},{5,6},{6,7},{7,8},{8,9},{9,10},{10,1... | collective-permute-start | bytes 9437192 | tf_op jit(solution)/shard_map/ppermute | solution.py:20
  26.6 1.9 all_gather.15
  29.1 1.3 collective-permute-start.1
  30.4 5.2 %collective-permute-start = (f32[6,8,256]{2,1,0:T(8,128)S(1)}, f32[6,8,256]{2,1,0:T(8,128)}, u32[]{:S(2)}, u32[]{:S(2)}) collective-permute-start(f32[6,8,256]{2,1,0:T(8,128)S(1)} %get-tuple-element.194), channel_id=1, source_target_pairs={{0,1},{1,2},{2,3},{3,4},{4,5},{5,6},{6,7},{7,8},{8,9},{9,10},{10,1... | collective-permute-start | bytes 147464 | tf_op jit(solution)/shard_map/ppermute | solution.py:20
  39.6 1.0 convert_element_type.41
  40.6 119.7 %collective-permute-done.1 = f32[6,8,256]{2,1,0:T(8,128)} collective-permute-done((f32[6,8,256]{2,1,0:T(8,128)}, f32[6,8,256]{2,1,0:T(8,128)}, u32[]{:S(2)}, u32[]{:S(2)}) %collective-permute-start.1) | collective-permute-done | bytes 49184 | tf_op jit(solution)/shard_map/ppermute | solution.py:23
  160.3 1.4 collective-permute-done
  161.7 1.1 select_maximum_fusion.2
  172.4 0.9 fusion.214
  173.4 9.2 %select_maximum_fusion = f32[64,6,32,260]{3,0,2,1:T(8,128)S(1)} fusion(f32[64,6,8,256]{3,0,2,1:T(8,128)} %collective-permute-done.3, f32[64,6,16,256]{3,0,2,1:T(8,128)S(1)} %bitcast.549, f32[64,6,8,256]{3,0,2,1:T(8,128)} %collective-permute-done.2), kind=kLoop, calls=%fused_computation.16 | loop fusion | flops 25559040 | bytes 25362432 | tf_op jit(solution)/shard_map/concatenate | solution.py:24
  182.6 6.6 %slice_bitcast_fusion = (f32[64,32,260]{2,0,1:T(8,128)}, f32[64,32,260]{2,0,1:T(8,128)}, f32[64,32,260]{2,0,1:T(8,128)}, f32[64,32,260]{2,0,1:T(8,128)}, f32[64,32,260]{2,0,1:T(8,128)}, /*index=5*/f32[64,32,260]{2,0,1:T(8,128)}) fusion(f32[64,6,32,260]{3,0,2,1:T(8,128)S(1)} %select_maximum_fusion), kind=kLoop, calls=%fused_computation.28 | loop fusion | bytes 25559040 | tf_op jit(solution)/shard_map/squeeze | solution.py:48
  189.3 2.2 multiply_subtract_fusion
  191.5 12.9 %multiply_add_fusion.3 = (f32[64,30,258]{2,0,1:T(8,128)S(1)}, f32[64,30,258]{2,0,1:T(8,128)}, f32[64,30,258]{2,0,1:T(8,128)S(1)}, f32[64,30,258]{2,0,1:T(8,128)S(1)}) fusion(f32[64,32,260]{2,0,1:T(8,128)} %get-tuple-element.85, f32[30,258]{1,0:T(8,128)S(1)} %copy-done.34, f32[30,258]{1,0:T(8,128)S(1)} %copy-done.36, f32[64,32,260]{2,0,1:T(8,128)} %get-tuple-element.82, ...), kind=kLoop, calls=%fused_computation.71 | loop fusion | flops 12879360 | bytes 21919680 | tf_op jit(solution)/shard_map/add | solution.py:84
  204.4 3.2 fusion.116
  207.6 1.8 fusion.111
  209.4 1.8 fusion.110
  211.2 0.9 copy-done.2
  212.1 6.3 %multiply_add_fusion.1 = (f32[64,30,258]{2,0,1:T(8,128)S(1)}, f32[64,30,258]{2,0,1:T(8,128)}, f32[64,30,258]{2,0,1:T(8,128)S(1)}, f32[64,30,258]{2,0,1:T(8,128)S(1)}) fusion(f32[64,32,260]{2,0,1:T(8,128)S(1)} %copy-done.2, f32[30,258]{1,0:T(8,128)S(1)} %copy-done.31, f32[30,258]{1,0:T(8,128)S(1)} %copy-done.32, f32[64,32,260]{2,0,1:T(8,128)S(1)} %copy-done.4, ...), kind=kLoop, calls=%fused_computation.69 | loop fusion | flops 12879360 | bytes 21919680 | tf_op jit(solution)/shard_map/add | solution.py:84
  218.4 3.3 fusion.109
  221.7 1.8 fusion.104
  223.5 1.8 fusion.103
  225.3 6.5 %broadcast_multiply_fusion = f32[64,6,28,256]{3,0,2,1:T(8,128)S(1)} fusion(f32[64,6,28,256]{3,0,2,1:T(8,128)} %fusion.103, f32[28]{0:T(128)S(1)} %copy-done.62), kind=kLoop, calls=%fused_computation.25 | loop fusion | flops 2752512 | bytes 22020208 | tf_op jit(solution)/shard_map/mul | solution.py:124
  231.8 6.7 %fusion.34 = (f32[64,28,260]{2,0,1:T(8,128)}, f32[64,28,260]{2,0,1:T(8,128)}, f32[64,28,260]{2,0,1:T(8,128)S(1)}, f32[64,28,260]{2,0,1:T(8,128)}, f32[64,28,260]{2,0,1:T(8,128)}, /*index=5*/f32[64,28,260]{2,0,1:T(8,128)S(1)}) fusion(f32[64,6,28,256]{3,0,2,1:T(8,128)S(1)} %broadcast_multiply_fusion), kind=kLoop, calls=%fused_computation.77 | loop fusion | bytes 22192128 | tf_op jit(solution)/shard_map/squeeze | solution.py:48
  238.5 2.9 multiply_subtract_fusion.1
  241.5 8.1 %multiply_add_fusion.7 = (f32[64,26,258]{2,0,1:T(8,128)S(1)}, f32[64,26,258]{2,0,1:T(8,128)}, f32[64,26,258]{2,0,1:T(8,128)S(1)}, f32[64,26,258]{2,0,1:T(8,128)}) fusion(f32[64,28,260]{2,0,1:T(8,128)S(1)} %get-tuple-element.101, f32[26,258]{1,0:T(8,128)S(1)} %copy-done.28, f32[26,258]{1,0:T(8,128)S(1)} %copy-done.30, f32[64,28,260]{2,0,1:T(8,128)} %get-tuple-element.99, ...), kind=kLoop, calls=%fused_computation.114 | loop fusion | flops 11162112 | bytes 18997056 | tf_op jit(solution)/shard_map/add | solution.py:84
  249.6 1.8 fusion.158
  254.1 5.8 %multiply_add_fusion.5 = (f32[64,26,258]{2,0,1:T(8,128)S(1)}, f32[64,26,258]{2,0,1:T(8,128)}, f32[64,26,258]{2,0,1:T(8,128)S(1)}, f32[64,26,258]{2,0,1:T(8,128)}) fusion(f32[64,28,260]{2,0,1:T(8,128)S(1)} %get-tuple-element.98, f32[26,258]{1,0:T(8,128)S(1)} %copy-done.25, f32[26,258]{1,0:T(8,128)S(1)} %copy-done.26, f32[64,28,260]{2,0,1:T(8,128)S(1)} %copy-done.7, ...), kind=kLoop, calls=%fused_computation.112 | loop fusion | flops 11162112 | bytes 18997056 | tf_op jit(solution)/shard_map/add | solution.py:84
  259.9 1.7 fusion.151
  262.1 1.2 copy-done.15
  263.8 2.1 broadcast_multiply_fusion.1
  265.9 4.0 fusion.68
  269.9 2.5 multiply_subtract_fusion.2
  272.4 5.8 %multiply_add_fusion.11 = (f32[64,22,258]{2,0,1:T(8,128)S(1)}, f32[64,22,258]{2,0,1:T(8,128)}, f32[64,22,258]{2,0,1:T(8,128)S(1)}, f32[64,22,258]{2,0,1:T(8,128)}) fusion(f32[64,24,260]{2,0,1:T(8,128)S(1)} %get-tuple-element.113, f32[22,258]{1,0:T(8,128)S(1)} %copy-done.44, f32[22,258]{1,0:T(8,128)} %get-tuple-element.185, ...), kind=kLoop, calls=%fused_computation.157 | loop fusion | flops 9444864 | bytes 16074432 | tf_op jit(solution)/shard_map/add | solution.py:84
  278.2 1.5 fusion.172
  280.2 1.1 copy-done.19
  281.8 3.9 multiply_add_fusion.9
  285.7 1.4 fusion.165
  287.9 1.3 broadcast_multiply_fusion.2
  289.2 7.0 %fusion.102 = (f32[64,20,260]{2,0,1:T(8,128)}, f32[64,20,260]{2,0,1:T(8,128)}, f32[64,20,260]{2,0,1:T(8,128)S(1)}, f32[64,20,260]{2,0,1:T(8,128)}, f32[64,20,260]{2,0,1:T(8,128)}, /*index=5*/f32[64,20,260]{2,0,1:T(8,128)}) fusion(f32[64,6,20,256]{3,0,2,1:T(8,128)S(1)} %broadcast_multiply_fusion.2), kind=kLoop, calls=%fused_computation.163 | loop fusion | bytes 15851520 | tf_op jit(solution)/shard_map/squeeze | solution.py:48
  296.2 2.1 multiply_subtract_fusion.3
  298.9 3.0 multiply_add_fusion.15
  302.0 1.2 fusion.186
  305.3 3.5 multiply_add_fusion.13
  308.8 1.2 fusion.179
  310.7 3.2 fusion.427
  313.9 2.7 copy-done.1
  317.5 0.9 gather_fusion
  318.6 1.9 all_gather.16
  320.4 0.9 fusion.463
  327.1 1.3 gather_fusion.1
  328.6 41.4 %psum.15 = f32[128]{0:T(128)S(1)} all-reduce(f32[128]{0:T(128)S(1)} %convolution_bitcast_fusion.2), channel_id=1, replica_groups=mesh['cols'=2,'space'=16] {'space'}, use_global_device_ids=true, to_apply=%region_3.4 | all-reduce | flops 128 | bytes 1024 | tf_op jit(solution)/shard_map/psum | solution.py:138
  370.0 55.5 %all-reduce.15.cloned.1.call-done = f32[128,128]{1,0:T(8,128)} async-done(((f32[128,128]{1,0:T(8,128)}), f32[128,128]{1,0:T(8,128)}) %all-reduce.15.cloned.1.call-update) | async-done | bytes 65552 | tf_op jit(solution)/shard_map/psum | solution.py:138
  425.5 0.9 convert_add_fusion
  426.5 0.9 fusion.193
  427.3 11.7 %cholesky.18 = f32[128,128]{1,0:T(8,128)S(1)} custom-call(f32[128,128]{1,0:T(8,128)S(1)} %fusion.193), custom_call_target="Cholesky" | custom-call | tf_op jit(solution)/shard_map/cholesky | solution.py:141
  440.4 9.8 %custom-call.9 = f32[1,128,128]{1,2,0:T(8,128)S(1)} custom-call(f32[1,128,128]{2,1,0:T(8,128)S(1)} %fusion.188), custom_call_target="InvertDiagBlocksLowerTriangular" | custom-call | tf_op jit(solution)/shard_map/triangular_solve | solution.py:143
  450.5 5.1 %fusion.409 = f32[1,6,16,256]{3,0,2,1:T(1,128)S(1)} fusion(f32[64,6,16,256]{3,0,2,1:T(8,128)} %copy-done.1, f32[128]{0:T(128)S(1)} %convolution_bitcast_fusion, s32[]{:T(128)S(6)} %select_n.47), kind=kOutput, calls=%fused_computation.722 | convolution fusion | flops 18874368 | bytes 6390276 | tf_op jit(solution)/shard_map/k,kfrc->frc/dot_general | solution.py:149
  455.7 2.1 all-gather
  458.8 3.8 fusion.397
  462.5 6.3 %copy.27 = f32[64,6,16,256]{3,2,1,0:T(8,128)} copy(f32[64,6,16,256]{3,0,2,1:T(8,128)S(1)} %fusion.397) | data formatting | bytes 12582912
  (251 shorter events, 32.6 us)
Async XLA Ops:
  8.0 417.5 %all-reduce.15.cloned.1.call-start = ((), (), s32[]{:S(2)}) async-start(), calls=%async_computation | async-start | bytes 131072 | tf_op jit(solution)/shard_map/psum | solution.py:138
  14.4 3.7 copy-start
  14.4 12.2 %copy-start.56 = (f32[6,16,128]{2,1,0:T(8,128)S(1)}, f32[6,16,128]{2,1,0:T(8,128)}, u32[]{:S(2)}) copy-start(f32[6,16,128]{2,1,0:T(8,128)} %param.6) | copy-start | bytes 147460
  14.4 21.1 %copy-start.67 = (s32[128]{0:T(128)S(1)}, s32[128]{0:T(128)}, u32[]{:S(2)}) copy-start(s32[128]{0:T(128)} %param.9) | copy-start | bytes 1540
  18.1 155.3 %collective-permute-start.3 = (f32[64,6,8,256]{3,0,2,1:T(8,128)}, f32[64,6,8,256]{3,0,2,1:T(8,128)}, u32[]{:S(2)}, u32[]{:S(2)}) collective-permute-start(f32[64,6,8,256]{3,0,2,1:T(8,128)} %get-tuple-element.129), channel_id=1, source_target_pairs={{1,0},{2,1},{3,2},{4,3},{5,4},{6,5},{7,6},{8,7},{9,8},{10,9},{11,1... | collective-permute-start | bytes 9437192 | tf_op jit(solution)/shard_map/ppermute | solution.py:23
  19.3 154.0 %collective-permute-start.2 = (f32[64,6,8,256]{3,0,2,1:T(8,128)S(1)}, f32[64,6,8,256]{3,0,2,1:T(8,128)}, u32[]{:S(2)}, u32[]{:S(2)}) collective-permute-start(f32[64,6,8,256]{3,0,2,1:T(8,128)S(1)} %get-tuple-element.128), channel_id=1, source_target_pairs={{0,1},{1,2},{2,3},{3,4},{4,5},{5,6},{6,7},{7,8},{8,9},{9,10},{10,1... | collective-permute-start | bytes 9437192 | tf_op jit(solution)/shard_map/ppermute | solution.py:20
  29.1 131.2 %collective-permute-start.1 = (f32[6,8,256]{2,1,0:T(8,128)}, f32[6,8,256]{2,1,0:T(8,128)}, u32[]{:S(2)}, u32[]{:S(2)}) collective-permute-start(f32[6,8,256]{2,1,0:T(8,128)} %get-tuple-element.195), channel_id=1, source_target_pairs={{1,0},{2,1},{3,2},{4,3},{5,4},{6,5},{7,6},{8,7},{9,8},{10,9},{11,1... | collective-permute-start | bytes 147464 | tf_op jit(solution)/shard_map/ppermute | solution.py:23
  30.4 131.3 %collective-permute-start = (f32[6,8,256]{2,1,0:T(8,128)S(1)}, f32[6,8,256]{2,1,0:T(8,128)}, u32[]{:S(2)}, u32[]{:S(2)}) collective-permute-start(f32[6,8,256]{2,1,0:T(8,128)S(1)} %get-tuple-element.194), channel_id=1, source_target_pairs={{0,1},{1,2},{2,3},{3,4},{4,5},{5,6},{6,7},{7,8},{8,9},{9,10},{10,1... | collective-permute-start | bytes 147464 | tf_op jit(solution)/shard_map/ppermute | solution.py:20
  40.6 123.2 %copy-start.61 = (f32[28]{0:T(128)S(1)}, f32[28]{0:T(128)}, u32[]{:S(2)}) copy-start(f32[28]{0:T(128)} %slice.1097) | copy-start | bytes 340
  161.7 11.7 %slice-start = ((s8[6291456]{0:T(1024)(128)(4,1)}), s8[4194304]{0:T(1024)(128)(4,1)S(1)}, s32[]{:S(2)}) async-start(s8[6291456]{0:T(1024)(128)(4,1)} %bitcast.548), calls=%async_computation.2 | async-start | bytes 8388608
  163.0 2.0 copy-start.64
  164.0 2.3 copy-start.60
  165.2 8.3 %slice-start.1 = ((s8[6291456]{0:T(1024)(128)(4,1)}), s8[2097152]{0:T(1024)(128)(4,1)S(1)}, s32[]{:S(2)}) async-start(s8[6291456]{0:T(1024)(128)(4,1)} %bitcast.548), calls=%async_computation.3 | async-start | bytes 4194304
  166.5 6.8 %copy-start.21 = (f32[20,260]{1,0:T(8,128)}, f32[20,260]{1,0:T(8,128)S(1)}, u32[]{:S(2)}) copy-start(f32[20,260]{1,0:T(8,128)S(1)} %get-tuple-element.173) | copy-start | bytes 62404
  166.5 6.8 %copy-start.24 = (f32[20,260]{1,0:T(8,128)}, f32[20,260]{1,0:T(8,128)S(1)}, u32[]{:S(2)}) copy-start(f32[20,260]{1,0:T(8,128)S(1)} %get-tuple-element.177) | copy-start | bytes 62404
  167.9 5.5 %copy-start.22 = (f32[18,258]{1,0:T(8,128)}, f32[18,258]{1,0:T(8,128)S(1)}, u32[]{:S(2)}) copy-start(f32[18,258]{1,0:T(8,128)S(1)} %get-tuple-element.12) | copy-start | bytes 55732
  167.9 5.5 %copy-start.37 = (f32[18,258]{1,0:T(8,128)}, f32[18,258]{1,0:T(8,128)S(1)}, u32[]{:S(2)}) copy-start(f32[18,258]{1,0:T(8,128)S(1)} %get-tuple-element.11) | copy-start | bytes 55732
  168.7 4.7 copy-start.38
  168.7 4.7 copy-start.39
  168.7 4.7 copy-start.40
  189.3 2.2 copy-start.34
  189.3 2.2 copy-start.35
  189.3 2.2 copy-start.36
  191.5 12.9 %copy-start.3 = (f32[64,32,260]{2,0,1:T(8,128)S(1)}, f32[64,32,260]{2,0,1:T(8,128)}, u32[]{:S(2)}) copy-start(f32[64,32,260]{2,0,1:T(8,128)} %get-tuple-element.85) | copy-start | bytes 6389764
  204.4 3.2 copy-start.10
  204.4 6.8 %copy-start.5 = (f32[64,32,260]{2,0,1:T(8,128)S(1)}, f32[64,32,260]{2,0,1:T(8,128)}, u32[]{:S(2)}) copy-start(f32[64,32,260]{2,0,1:T(8,128)} %get-tuple-element.81) | copy-start | bytes 6389764
  207.6 3.6 copy-start.4
  209.4 2.7 copy-start.2
  209.4 2.7 copy-start.31
  209.4 2.7 copy-start.32
  209.4 2.7 copy-start.33
  218.4 3.3 copy-start.9
  238.5 2.9 copy-start.28
  238.5 2.9 copy-start.29
  238.5 2.9 copy-start.30
  249.6 2.5 copy-start.16
  251.4 1.9 copy-start.7
  251.4 2.7 copy-start.8
  251.4 2.7 copy-start.25
  251.4 2.7 copy-start.26
  251.4 2.7 copy-start.27
  269.9 2.5 copy-start.44
  269.9 2.5 copy-start.45
  279.8 1.9 copy-start.42
  279.8 1.9 copy-start.43
  296.2 2.1 copy-start.6
  296.2 2.1 copy-start.13
  296.2 2.7 copy-start.14
  296.2 2.7 copy-start.23
  296.2 2.7 copy-start.49
  296.2 2.7 copy-start.50
  296.2 2.7 copy-start.51
  303.2 2.1 copy-start.12
  303.2 2.1 copy-start.46
  303.2 2.1 copy-start.47
  303.2 2.1 copy-start.48
  313.9 2.7 copy-start.1
  317.4 4.5 copy-start.54
  317.4 4.5 copy-start.55
  317.4 7.0 %copy-start.52 = (f32[18,258]{1,0:T(8,128)S(1)}, f32[18,258]{1,0:T(8,128)}, u32[]{:S(2)}) copy-start(f32[18,258]{1,0:T(8,128)} %get-tuple-element.10) | copy-start | bytes 55732
  317.4 7.0 %copy-start.53 = (f32[18,258]{1,0:T(8,128)S(1)}, f32[18,258]{1,0:T(8,128)}, u32[]{:S(2)}) copy-start(f32[18,258]{1,0:T(8,128)} %get-tuple-element.13) | copy-start | bytes 55732
  317.4 11.0 %copy-start.58 = (s32[128]{0:T(128)S(1)}, s32[128]{0:T(128)}, u32[]{:S(2)}) copy-start(s32[128]{0:T(128)} %copy-done.57) | copy-start | bytes 1540
  317.5 11.0 %copy-start.66 = (f32[128]{0:T(128)S(1)}, f32[128]{0:T(128)}, u32[]{:S(2)}) copy-start(f32[128]{0:T(128)} %param.10) | copy-start | bytes 1540
  321.3 137.4 %all-gather.3.cloned.1.call-start = ((), (), s32[]{:S(2)}) async-start(), calls=%async_computation.1 | async-start | bytes 9437184 | tf_op jit(solution)/shard_map/all_gather | solution.py:155
  (12 other events, 18.5 us)
Sparse Core Ops, SparseCore 0:
  321.4 104.0 all-reduce.14
Sparse Core Ops, SparseCore 1:
  323.3 17.2 all-gather.2
